TPU v7x, 512 devices: a whole 4x4x16 slice. The times are simulated.
512 devices in a mesh: ifg: 128 (over x, z, core), tile: 4 (over y).
Axes of the slice: x: 4, y: 4, z: 16, core: 2. Of those that a mesh axis runs over, the one named last changes fastest.
Arguments:
- ifgs: bfloat16 [1152, 8, 16384], P('ifg', 'tile'), may hold values from -12 to 12
- pairs: int32 [1152, 2], replicated, may hold values from 0 to 299, as said below
- pseudo_inverse: bfloat16 [300, 1152], P(None, 'ifg'), may hold values from -0.1875 to 0.1875
- ref_pixels: int32 [64], replicated, may hold values from 0 to 131071
- epochs: int32 [8], replicated, may hold values from 8 to 291
Outputs:
- coefficients: float32 [16, 8, 16384], P(None, 'tile', 'ifg')
- misfit_rms: float32 [8, 16384], P('tile', 'ifg')
Inputs may be any that keep to these rules, and one draw needn't show every extreme that they name: pairs[k, 0] < pairs[k, 1] <= pairs[k, 0] + 6.
All inputs are finite; a program needn't handle non-finite values.
Results may differ from a plain program's by a relative error of at most 0.0029.
Values may be sent and summed in bfloat16 or wider, within the bound.
A program may use at most 64 MiB of HBM per device.

v0:
```python
import math
import jax
import jax.numpy as jnp
from jax import lax
from jax.sharding import PartitionSpec as P

EPS = 1e-06
RIDGE = 1.0


def design(epochs, count):
    index = jnp.arange(count, dtype=jnp.int32)
    days = index.astype(jnp.float32)
    scaled = 2.0 * days / (count - 1) - 1.0
    years = days * 12.0 / 365.25
    smooth = jnp.stack(
        [
            jnp.ones_like(days),
            scaled,
            scaled * scaled,
            scaled * scaled * scaled,
            jnp.sin(2.0 * math.pi * years),
            jnp.cos(2.0 * math.pi * years),
            jnp.sin(4.0 * math.pi * years),
            jnp.cos(4.0 * math.pi * years),
        ],
        axis=1,
    )
    jumps = (index[:, None] >= epochs[None, :]).astype(jnp.float32)
    return jnp.concatenate([smooth, jumps], axis=1)


def fit_operator(epochs, count):
    matrix = design(epochs, count)
    normal = jnp.dot(
        matrix.T, matrix, precision=lax.Precision.HIGHEST, preferred_element_type=jnp.float32
    )
    normal = normal + RIDGE * jnp.eye(matrix.shape[1], dtype=jnp.float32)
    factor = jnp.linalg.cholesky(normal)
    return jax.scipy.linalg.cho_solve((factor, True), matrix.T)


def incidence_matrix(pairs, count):
    dates = jnp.arange(count, dtype=jnp.int32)
    later = (pairs[:, 1:2] == dates[None, :]).astype(jnp.float32)
    earlier = (pairs[:, 0:1] == dates[None, :]).astype(jnp.float32)
    return later - earlier


def shards(ifgs, pairs, pseudo_inverse, ref_pixels, epochs):
    row_count = ifgs.shape[1]
    col_total = ifgs.shape[2]
    col_count = col_total // lax.axis_size("ifg")
    region_size = ref_pixels.shape[0]
    date_count = pseudo_inverse.shape[0]
    tile_index = lax.axis_index("tile")
    ifg_index = lax.axis_index("ifg")
    ref_row = ref_pixels // col_total
    ref_col = ref_pixels % col_total
    row_rel = ref_row - tile_index * row_count
    in_tile = (row_rel >= 0) & (row_rel < row_count)
    row_safe = jnp.clip(row_rel, 0, row_count - 1)
    regrouped = lax.all_to_all(ifgs, "ifg", split_axis=2, concat_axis=0, tiled=True)
    col_rel = ref_col - ifg_index * col_count
    in_block = in_tile & (col_rel >= 0) & (col_rel < col_count)
    col_safe = jnp.clip(col_rel, 0, col_count - 1)
    values = regrouped[:, row_safe, col_safe].astype(jnp.float32)
    partial_value = jnp.sum(jnp.where(in_block[None, :], values, 0.0), axis=1)
    totals = lax.psum(partial_value, ("ifg", "tile"))
    corrected = (regrouped.astype(jnp.float32) - (totals / region_size)[:, None, None]).astype(
        jnp.bfloat16
    )
    pixel_rows = corrected.reshape(corrected.shape[0], row_count * col_count)
    displacement = jnp.dot(
        lax.all_gather(pseudo_inverse, "ifg", axis=1, tiled=True),
        pixel_rows,
        preferred_element_type=jnp.float32,
    )
    operator = fit_operator(epochs, date_count)
    coeffs = jnp.dot(
        operator, displacement, precision=lax.Precision.HIGHEST, preferred_element_type=jnp.float32
    )
    incidence = incidence_matrix(pairs, date_count)
    predicted = jnp.dot(
        incidence, displacement, precision=lax.Precision.HIGHEST, preferred_element_type=jnp.float32
    )
    misfit = pixel_rows.astype(jnp.float32) - predicted
    spread = jnp.sqrt(jnp.mean(misfit * misfit, axis=0) + EPS)
    return (
        coeffs.reshape(operator.shape[0], row_count, col_count),
        spread.reshape(row_count, col_count),
    )


def solution(mesh):
    in_specs = (P("ifg", "tile", None), P(), P(None, "ifg"), P(), P())
    out_specs = (P(None, "tile", "ifg"), P("tile", "ifg"))
    return jax.shard_map(shards, mesh=mesh, in_specs=in_specs, out_specs=out_specs, check_vma=False)
```

profile of v0, /device:TPU:1, one launch (start us, length us, event | category | flops | bytes accessed | tf_op | source)
XLA Modules:
  0.0 324.9 jit_solution(13141437848219759013)
XLA Ops:
  0.6 15.8 %copy.18 = bf16[9,2,16384]{0,1,2:T(2,128)(2,1)} copy(bf16[9,2,16384]{2,1,0:T(2,128)(2,1)} %param.5) | data formatting | bytes 1179648 | tf_op args[0]
  16.4 18.2 %reshape.101 = bf16[128,2,1152]{2,1,0:T(2,128)(2,1)} reshape(bf16[16384,2,9]{2,1,0:T(2,128)(2,1)} %bitcast.43) | data formatting | bytes 1179648
  34.7 20.5 %all-to-all-start = ((bf16[128,2,1152]{2,1,0:T(2,128)(2,1)}), bf16[128,2,1152]{2,1,0:T(2,128)(2,1)S(1)}, u32[]{:S(2)}, u32[]{:S(2)}) async-start(bf16[128,2,1152]{2,1,0:T(2,128)(2,1)} %reshape.101), calls=%async_computation | async-start | bytes 1179648 | tf_op jit(solution)/shard_map/all_to_all | solution.py:63
  55.2 0.1 fusion.19
  55.3 0.1 fusion.21
  55.4 0.1 multiply_add_fusion
  55.5 0.0 copy-done.2
  55.5 0.1 fusion.10
  55.6 0.2 fusion.35
  55.7 0.1 copy.17
  55.8 1.5 cholesky.17
  57.3 0.6 compare_reduce_fusion
  57.9 0.6 fusion.11
  58.6 1.2 custom-call.10
  59.8 118.4 %all-gather = bf16[128,9,300]{2,1,0:T(8,128)(2,1)S(1)} all-gather(bf16[1,9,300]{2,1,0:T(8,128)(2,1)S(1)} %bitcast.47), channel_id=1, replica_groups=mesh['ifg'=128,'tile'=4] {'ifg'}, dimensions={0}, use_global_device_ids=true | all-gather | bytes 696600 | tf_op jit(solution)/shard_map/all_gather | solution.py:75
  178.2 0.7 reshape.98
  178.9 0.0 copy-done.1
  179.0 0.2 fusion.14
  179.2 0.2 fusion.12
  179.4 0.0 all-to-all-done
  179.4 19.3 %reshape.102 = bf16[16384,2,9]{2,1,0:T(2,128)(2,1)} reshape(bf16[128,2,1152]{2,1,0:T(2,128)(2,1)S(1)} %all-to-all-done) | data formatting | bytes 1179648
  198.7 16.6 %copy.19 = bf16[9,2,128,128]{3,1,0,2:T(2,128)(2,1)S(1)} copy(bf16[9,2,128,128]{0,1,3,2:T(2,128)(2,1)} %bitcast.42) | data formatting | bytes 1179648 | tf_op jit(solution)/shard_map/all_to_all | solution.py:63
  215.2 0.4 bitcast_convert_fusion
  215.7 0.6 copy.20
  216.3 1.2 gather_fusion
  217.5 0.1 select_reduce_fusion
  217.6 102.6 %psum.7 = f32[1152]{0:T(1024)S(1)} all-reduce(f32[1152]{0:T(1024)S(1)} %select_reduce_fusion), channel_id=1, replica_groups=mesh['ifg'=128,'tile'=4] {'ifg','tile'}, use_global_device_ids=true, to_apply=%region_3.4 | all-reduce | flops 1152 | bytes 9216 | tf_op jit(solution)/shard_map/psum | solution.py:69
  320.1 0.7 fusion.31
  320.8 0.2 fusion.36
  321.0 0.7 reshape.77
  321.7 2.6 fusion.4
  324.4 0.6 sqrt_bitcast_fusion
  (15 shorter events, 0.2 us)
Async XLA Ops:
  34.7 20.8 %copy-start.2 = (s32[8]{0:T(128)S(1)}, s32[8]{0:T(128)}, u32[]{:S(2)}) copy-start(s32[8]{0:T(128)} %param.9) | copy-start | bytes 100
  34.7 25.2 %copy-start = (bf16[300,9]{0,1:T(8,128)(2,1)S(1)}, bf16[300,9]{0,1:T(8,128)(2,1)}, u32[]{:S(2)}) copy-start(bf16[300,9]{0,1:T(8,128)(2,1)} %param.7) | copy-start | bytes 16204
  34.7 144.7 %all-to-all-start = ((bf16[128,2,1152]{2,1,0:T(2,128)(2,1)}), bf16[128,2,1152]{2,1,0:T(2,128)(2,1)S(1)}, u32[]{:S(2)}, u32[]{:S(2)}) async-start(bf16[128,2,1152]{2,1,0:T(2,128)(2,1)} %reshape.101), calls=%async_computation | async-start | bytes 1179648 | tf_op jit(solution)/shard_map/all_to_all | solution.py:63
  178.2 0.7 copy-start.1
  178.2 0.7 copy-start.3
where the time goes:
time: 327 us; the launch traced here: 325 us
  blocking collectives  221 us (68%)
  local copies, waits for them, and re-layouts  73.1 us (22%)
  starting transfers between devices  20.5 us (6%)
  other arithmetic  5.45 us (2%)
  matrix products  4.07 us (1%)
    all_gather x1, blocking collectives, shards(): lax.all_gather(pseudo_inverse, 'ifg', axis=1, tiled=True)  118 us
    psum x1, blocking collectives, shards(): totals = lax.psum(partial_value, ('ifg', 'tile'))  103 us
    unnamed x12, local copies, waits for them, and re-layouts  54 us
    all_to_all x1, starting transfers between devices, shards(): lax.all_to_all(ifgs, 'ifg', split_axis=2, concat_axis=0, tiled=True)  20.5 us
    all_to_all x2, local copies, waits for them, and re-layouts, shards(): lax.all_to_all(ifgs, 'ifg', split_axis=2, concat_axis=0, tiled=True)  17.2 us
  transfers between devices with their start and end apart: 1, of which 0 were waited for; matrix products, arithmetic and copies ran while one was open for 2% of the time, Pallas kernels for 0%

commit v1 on v0

--- a/solution.py
+++ b/solution.py
@@ -72,7 +72,9 @@
     )
     pixel_rows = corrected.reshape(corrected.shape[0], row_count * col_count)
     displacement = jnp.dot(
-        lax.all_gather(pseudo_inverse, "ifg", axis=1, tiled=True),
+        jnp.concatenate(
+            lax.all_to_all(jnp.stack([pseudo_inverse] * lax.axis_size("ifg")), "ifg", 0, 0), axis=1
+        ),
         pixel_rows,
         preferred_element_type=jnp.float32,
     )

time: 327 us -> 261 us (0.80)
  blocking collectives: 221 us -> 106 us
  waiting for transfers between devices: 0.01 us -> 32.5 us
  starting transfers between devices: 20.5 us -> 27.9 us
  local copies, waits for them, and re-layouts: 73.1 us -> 78.5 us
  other arithmetic: 5.45 us -> 8.85 us
    all_gather x1 -> x0, blocking collectives: 118 us -> none  [shards(): lax.all_gather(pseudo_inverse, 'ifg', axis=1, tiled=True)]
    all_to_all x1, waiting for transfers between devices: 0.01 us -> 32.5 us  [shards(): lax.all_to_all(ifgs, 'ifg', split_axis=2, concat_axis=0, tiled=True)]
    all_to_all x0 -> x1, starting transfers between devices: none -> 7.55 us  [shards(): lax.all_to_all(jnp.stack([pseudo_inverse] * lax.axis_size('ifg')), 'ifg',...]
    unnamed x12 -> x18, local copies, waits for them, and re-layouts: 54 us -> 58.3 us
    psum x1, blocking collectives: 103 us -> 106 us  [shards(): totals = lax.psum(partial_value, ('ifg', 'tile'))]
  transfers between devices with their start and end apart: 1 -> 2, of which waited for: 0 -> 1; matrix products, arithmetic and copies ran while one was open for 2% -> 19% of each run, Pallas kernels for 0% -> 0%
where the time goes in v1:
time: 261 us; the launch traced here: 259 us
  blocking collectives  106 us (41%)
  local copies, waits for them, and re-layouts  78.5 us (30%)
  waiting for transfers between devices  32.5 us (12%)
  starting transfers between devices  27.9 us (11%)
  other arithmetic  8.85 us (3%)
  matrix products  3.87 us (1%)
    psum x1, blocking collectives, shards(): totals = lax.psum(partial_value, ('ifg', 'tile'))  106 us
    unnamed x18, local copies, waits for them, and re-layouts  58.3 us
    all_to_all x1, waiting for transfers between devices, shards(): lax.all_to_all(ifgs, 'ifg', split_axis=2, concat_axis=0, tiled=True)  32.5 us
    all_to_all x1, starting transfers between devices, shards(): lax.all_to_all(ifgs, 'ifg', split_axis=2, concat_axis=0, tiled=True)  20.4 us
    all_to_all x2, local copies, waits for them, and re-layouts, shards(): lax.all_to_all(ifgs, 'ifg', split_axis=2, concat_axis=0, tiled=True)  17.2 us
    all_to_all x1, starting transfers between devices, shards(): lax.all_to_all(jnp.stack([pseudo_inverse] * lax.axis_size('ifg')), 'ifg',...  7.55 us
  transfers between devices with their start and end apart: 2, of which 1 were waited for; matrix products, arithmetic and copies ran while one was open for 19% of the time, Pallas kernels for 0%

profile of v1, /device:TPU:1, one launch (start us, length us, event | category | flops | bytes accessed | tf_op | source)
XLA Modules:
  0.0 258.8 jit_solution(2375770332111473166)
XLA Ops:
  0.6 15.8 %copy.19 = bf16[9,2,16384]{0,1,2:T(2,128)(2,1)} copy(bf16[9,2,16384]{2,1,0:T(2,128)(2,1)} %param.5) | data formatting | bytes 1179648 | tf_op args[0]
  16.4 18.2 %reshape.117 = bf16[128,2,1152]{2,1,0:T(2,128)(2,1)} reshape(bf16[16384,2,9]{2,1,0:T(2,128)(2,1)} %bitcast.54) | data formatting | bytes 1179648
  34.7 20.4 %all-to-all-start = ((bf16[128,2,1152]{2,1,0:T(2,128)(2,1)}), bf16[128,2,1152]{2,1,0:T(2,128)(2,1)S(1)}, u32[]{:S(2)}, u32[]{:S(2)}) async-start(bf16[128,2,1152]{2,1,0:T(2,128)(2,1)} %reshape.117), calls=%async_computation | async-start | bytes 1179648 | tf_op jit(solution)/shard_map/all_to_all | solution.py:63
  55.1 0.1 broadcast_bitcast_fusion
  55.3 2.6 reshape.115
  58.2 32.5 %all-to-all-done = bf16[128,2,1152]{2,1,0:T(2,128)(2,1)S(1)} async-done(((bf16[128,2,1152]{2,1,0:T(2,128)(2,1)}), bf16[128,2,1152]{2,1,0:T(2,128)(2,1)S(1)}, u32[]{:S(2)}, u32[]{:S(2)}) %all-to-all-start) | async-done | bytes 589856 | tf_op jit(solution)/shard_map/all_to_all | solution.py:63
  90.7 7.6 %all-to-all-start.1 = ((bf16[128,2,1350]{2,1,0:T(2,128)(2,1)}), bf16[128,2,1350]{2,1,0:T(2,128)(2,1)S(1)}, u32[]{:S(2)}, u32[]{:S(2)}) async-start(bf16[128,2,1350]{2,1,0:T(2,128)(2,1)} %reshape.115), calls=%async_computation.1 | async-start | bytes 1441792 | tf_op jit(solution)/shard_map/all_to_all | solution.py:76
  98.3 0.1 fusion.36
  98.5 1.5 cholesky.17
  100.0 0.6 compare_reduce_fusion
  100.6 0.6 fusion.14
  101.3 1.2 custom-call.10
  102.6 0.2 fusion.17
  102.9 0.2 fusion.15
  103.0 19.3 %reshape.118 = bf16[16384,2,9]{2,1,0:T(2,128)(2,1)} reshape(bf16[128,2,1152]{2,1,0:T(2,128)(2,1)S(1)} %all-to-all-done) | data formatting | bytes 1179648
  122.3 16.6 %copy.20 = bf16[9,2,128,128]{3,1,0,2:T(2,128)(2,1)S(1)} copy(bf16[9,2,128,128]{0,1,3,2:T(2,128)(2,1)} %bitcast.53) | data formatting | bytes 1179648 | tf_op jit(solution)/shard_map/all_to_all | solution.py:63
  138.9 0.6 copy.21
  139.5 1.2 gather_fusion
  140.7 0.1 select_reduce_fusion
  140.8 106.2 %psum.7 = f32[1152]{0:T(1024)S(1)} all-reduce(f32[1152]{0:T(1024)S(1)} %select_reduce_fusion), channel_id=1, replica_groups=mesh['ifg'=128,'tile'=4] {'ifg','tile'}, use_global_device_ids=true, to_apply=%region_3.4 | all-reduce | flops 1152 | bytes 9216 | tf_op jit(solution)/shard_map/psum | solution.py:69
  247.0 0.2 sub.54
  247.2 2.4 subtract_convert_fusion
  249.6 1.4 bitcast_convert_fusion
  251.0 1.9 reshape.116
  253.0 0.2 bitcast_bitcast_fusion
  253.1 0.7 reshape.92
  253.8 0.4 copy-done.1
  254.2 0.5 fusion.10
  254.7 0.2 fusion.37
  254.9 0.7 reshape.93
  255.5 2.7 %fusion.4 = f32[256]{0:T(256)S(1)} fusion(f32[256,300]{0,1:T(8,128)S(1)} %fusion.10, s32[1152]{0:T(1024)S(1)} %get-tuple-element.3, s32[1152]{0:T(1024)S(1)} %get-tuple-element.2, f32[144,8,2,128]{3,2,1,0:T(2,128)S(1)} %bitcast.57, f32[1152]{0:T(1024)S(1)} %broadcast_multiply_fusion), kind=kOutput, calls=%fused_computation.8 | convolution fusion | flops 1065180416 | bytes 1501696 | tf_op jit(solution)/shard_map/dot_general | solution.py:86
  258.2 0.6 sqrt_bitcast_fusion
  (26 shorter events, 0.6 us)
Async XLA Ops:
  0.6 54.4 %copy-start = (bf16[300,9]{0,1:T(8,128)(2,1)S(1)}, bf16[300,9]{0,1:T(8,128)(2,1)}, u32[]{:S(2)}) copy-start(bf16[300,9]{0,1:T(8,128)(2,1)} %param.7) | copy-start | bytes 16204
  34.7 56.0 %all-to-all-start = ((bf16[128,2,1152]{2,1,0:T(2,128)(2,1)}), bf16[128,2,1152]{2,1,0:T(2,128)(2,1)S(1)}, u32[]{:S(2)}, u32[]{:S(2)}) async-start(bf16[128,2,1152]{2,1,0:T(2,128)(2,1)} %reshape.117), calls=%async_computation | async-start | bytes 1179648 | tf_op jit(solution)/shard_map/all_to_all | solution.py:63
  55.1 3.0 %copy-start.4 = (s32[8]{0:T(128)S(1)}, s32[8]{0:T(128)}, u32[]{:S(2)}) copy-start(s32[8]{0:T(128)} %param.9) | copy-start | bytes 100
  55.2 47.3 %copy-start.3 = (s32[1152,2]{0,1:T(2,128)S(1)}, s32[1152,2]{0,1:T(2,128)}, u32[]{:S(2)}) copy-start(s32[1152,2]{0,1:T(2,128)} %param.6) | copy-start | bytes 27652
  55.2 47.3 %copy-start.5 = (s32[64]{0:T(128)S(1)}, s32[64]{0:T(128)}, u32[]{:S(2)}) copy-start(s32[64]{0:T(128)} %param.8) | copy-start | bytes 772
  90.7 160.3 %all-to-all-start.1 = ((bf16[128,2,1350]{2,1,0:T(2,128)(2,1)}), bf16[128,2,1350]{2,1,0:T(2,128)(2,1)S(1)}, u32[]{:S(2)}, u32[]{:S(2)}) async-start(bf16[128,2,1350]{2,1,0:T(2,128)(2,1)} %reshape.115), calls=%async_computation.1 | async-start | bytes 1441792 | tf_op jit(solution)/shard_map/all_to_all | solution.py:76
  253.1 1.1 copy-start.1
  253.8 1.7 copy-start.2

commit v2 on v0

--- a/solution.py
+++ b/solution.py
@@ -66,7 +66,7 @@
     col_safe = jnp.clip(col_rel, 0, col_count - 1)
     values = regrouped[:, row_safe, col_safe].astype(jnp.float32)
     partial_value = jnp.sum(jnp.where(in_block[None, :], values, 0.0), axis=1)
-    totals = lax.psum(partial_value, ("ifg", "tile"))
+    totals = lax.psum(lax.psum(partial_value, "tile"), "ifg")
     corrected = (regrouped.astype(jnp.float32) - (totals / region_size)[:, None, None]).astype(
         jnp.bfloat16
     )

time: 327 us -> 486 us (1.49)
  blocking collectives: 221 us -> 380 us
    psum x1 -> x2, blocking collectives: 103 us -> 261 us  [shards(): totals = lax.psum(lax.psum(partial_value, 'tile'), 'ifg')]
  transfers between devices with their start and end apart: 1 -> 1, of which waited for: 0 -> 0; matrix products, arithmetic and copies ran while one was open for 2% -> 1% of each run, Pallas kernels for 0% -> 0%
where the time goes in v2:
time: 486 us; the launch traced here: 484 us
  blocking collectives  380 us (78%)
  local copies, waits for them, and re-layouts  73.1 us (15%)
  starting transfers between devices  20.5 us (4%)
  other arithmetic  5.45 us (1%)
    psum x2, blocking collectives, shards(): totals = lax.psum(lax.psum(partial_value, 'tile'), 'ifg')  261 us
    all_gather x1, blocking collectives, shards(): lax.all_gather(pseudo_inverse, 'ifg', axis=1, tiled=True)  118 us
    unnamed x12, local copies, waits for them, and re-layouts  54 us
    all_to_all x1, starting transfers between devices, shards(): lax.all_to_all(ifgs, 'ifg', split_axis=2, concat_axis=0, tiled=True)  20.5 us
    all_to_all x2, local copies, waits for them, and re-layouts, shards(): lax.all_to_all(ifgs, 'ifg', split_axis=2, concat_axis=0, tiled=True)  17.2 us
  transfers between devices with their start and end apart: 1, of which 0 were waited for; matrix products, arithmetic and copies ran while one was open for 1% of the time, Pallas kernels for 0%

profile of v2, /device:TPU:1, one launch (start us, length us, event | category | flops | bytes accessed | tf_op | source)
XLA Modules:
  0.0 483.6 jit_solution(12632343201989399949)
XLA Ops:
  0.6 15.8 %copy.18 = bf16[9,2,16384]{0,1,2:T(2,128)(2,1)} copy(bf16[9,2,16384]{2,1,0:T(2,128)(2,1)} %param.5) | data formatting | bytes 1179648 | tf_op args[0]
  16.4 18.2 %reshape.101 = bf16[128,2,1152]{2,1,0:T(2,128)(2,1)} reshape(bf16[16384,2,9]{2,1,0:T(2,128)(2,1)} %bitcast.43) | data formatting | bytes 1179648
  34.7 20.5 %all-to-all-start = ((bf16[128,2,1152]{2,1,0:T(2,128)(2,1)}), bf16[128,2,1152]{2,1,0:T(2,128)(2,1)S(1)}, u32[]{:S(2)}, u32[]{:S(2)}) async-start(bf16[128,2,1152]{2,1,0:T(2,128)(2,1)} %reshape.101), calls=%async_computation | async-start | bytes 1179648 | tf_op jit(solution)/shard_map/all_to_all | solution.py:63
  55.2 0.1 fusion.19
  55.3 0.1 fusion.21
  55.4 0.1 multiply_add_fusion
  55.5 0.1 fusion.10
  55.6 0.2 fusion.35
  55.7 0.1 copy.17
  55.8 1.5 cholesky.17
  57.3 0.6 compare_reduce_fusion
  57.9 0.6 fusion.11
  58.6 1.2 custom-call.10
  59.8 118.4 %all-gather = bf16[128,9,300]{2,1,0:T(8,128)(2,1)S(1)} all-gather(bf16[1,9,300]{2,1,0:T(8,128)(2,1)S(1)} %bitcast.47), channel_id=1, replica_groups=mesh['ifg'=128,'tile'=4] {'ifg'}, dimensions={0}, use_global_device_ids=true | all-gather | bytes 696600 | tf_op jit(solution)/shard_map/all_gather | solution.py:75
  178.2 0.7 reshape.98
  178.9 0.0 copy-done.1
  179.0 0.2 fusion.14
  179.2 0.2 fusion.12
  179.4 0.0 all-to-all-done
  179.4 19.3 %reshape.102 = bf16[16384,2,9]{2,1,0:T(2,128)(2,1)} reshape(bf16[128,2,1152]{2,1,0:T(2,128)(2,1)S(1)} %all-to-all-done) | data formatting | bytes 1179648
  198.7 16.6 %copy.19 = bf16[9,2,128,128]{3,1,0,2:T(2,128)(2,1)S(1)} copy(bf16[9,2,128,128]{0,1,3,2:T(2,128)(2,1)} %bitcast.42) | data formatting | bytes 1179648 | tf_op jit(solution)/shard_map/all_to_all | solution.py:63
  215.2 0.4 bitcast_convert_fusion
  215.7 0.6 copy.20
  216.3 1.2 gather_fusion
  217.5 0.1 select_reduce_fusion
  217.6 8.8 %psum.14 = f32[1152]{0:T(1024)S(1)} all-reduce(f32[1152]{0:T(1024)S(1)} %select_reduce_fusion), channel_id=1, replica_groups=mesh['ifg'=128,'tile'=4] {'tile'}, use_global_device_ids=true, to_apply=%region_3.4 | all-reduce | flops 1152 | bytes 9216 | tf_op jit(solution)/shard_map/psum | solution.py:69
  226.4 252.4 %psum.15 = f32[1152]{0:T(1024)S(1)} all-reduce(f32[1152]{0:T(1024)S(1)} %psum.14), channel_id=1, replica_groups=mesh['ifg'=128,'tile'=4] {'ifg'}, use_global_device_ids=true, to_apply=%region_4.5 | all-reduce | flops 1152 | bytes 9216 | tf_op jit(solution)/shard_map/psum | solution.py:69
  478.8 0.7 fusion.31
  479.5 0.2 fusion.36
  479.7 0.7 reshape.77
  480.4 2.6 fusion.4
  483.1 0.6 sqrt_bitcast_fusion
  (16 shorter events, 0.2 us)
Async XLA Ops:
  34.7 20.8 %copy-start.2 = (s32[8]{0:T(128)S(1)}, s32[8]{0:T(128)}, u32[]{:S(2)}) copy-start(s32[8]{0:T(128)} %param.9) | copy-start | bytes 100
  34.7 25.2 %copy-start = (bf16[300,9]{0,1:T(8,128)(2,1)S(1)}, bf16[300,9]{0,1:T(8,128)(2,1)}, u32[]{:S(2)}) copy-start(bf16[300,9]{0,1:T(8,128)(2,1)} %param.7) | copy-start | bytes 16204
  34.7 144.7 %all-to-all-start = ((bf16[128,2,1152]{2,1,0:T(2,128)(2,1)}), bf16[128,2,1152]{2,1,0:T(2,128)(2,1)S(1)}, u32[]{:S(2)}, u32[]{:S(2)}) async-start(bf16[128,2,1152]{2,1,0:T(2,128)(2,1)} %reshape.101), calls=%async_computation | async-start | bytes 1179648 | tf_op jit(solution)/shard_map/all_to_all | solution.py:63
  178.2 0.7 copy-start.1
  178.2 0.7 copy-start.3
